TPU v7x, 32 devices: a whole 2x2x4 slice. The times are simulated.
32 devices in a mesh: gx: 4 (over y, x), gy: 2 (over core), gz: 4 (over z).
Axes of the slice: x: 2, y: 2, z: 4, core: 2. Of those that a mesh axis runs over, the one named last changes fastest.
Arguments:
- thermal_field: float32 [32, 32, 512], P('gz', 'gy', 'gx'), may hold values from -2 to 4
- forcing_per_step: float32 [32, 32, 512], P('gz', 'gy', 'gx'), may hold values from 0.1 to 4
- substance_label: int32 [32, 32, 512], P('gz', 'gy', 'gx'), may hold values from 0 to 7
- thermal_conductivities: float32 [8], replicated, may hold values from 0.5 to 4
- patch_group_label: int32 [4, 4, 16], P('gz', 'gy', 'gx'), may hold values from 0 to 63, as said below
- drain_power_density: float32 [64], replicated, may hold values from 0.2 to 2
Outputs:
- next_thermal_field: float32 [32, 32, 512], P('gz', 'gy', 'gx')
- forcing_with_drain: float32 [32, 32, 512], P('gz', 'gy', 'gx')
Inputs may be any that keep to these rules, and one draw needn't show every extreme that they name: `patch_group_label`: every cluster labels exactly four tiles.
All inputs are finite; a program needn't handle non-finite values.
Results may differ from a plain program's by a relative error of at most 0.0003.
Values sent between devices are 32-bit elements; how exact they have to be, the bound alone decides.
A program may use at most 64 MiB of HBM per device.

v0:
```python
import jax
import jax.numpy as jnp
from jax import lax
from jax.sharding import PartitionSpec as P

TX = 32
TY = 8
IMPLICIT_WEIGHT = 0.5
LATERAL_RATE = 100.0
VERTICAL_RATE = 400.0
SOURCE_STEP = 0.5
LEAK_SLOPE = 0.5


def padded(shard, sides, width):
    for axis, dim in sides:
        devices, length = (lax.axis_size(axis), shard.shape[dim])
        up = [(i, (i + 1) % devices) for i in range(devices - 1)]
        down = [(j, i) for i, j in up]
        last = lax.slice_in_dim(shard, length - width, length, axis=dim)
        first = lax.slice_in_dim(shard, 0, width, axis=dim)
        before = lax.ppermute(last, axis, up)
        after = lax.ppermute(first, axis, down)
        shard = jnp.concatenate([before, shard, after], axis=dim)
    return shard


def harmonic(first_k, second_k):
    return 2.0 * first_k * second_k / (first_k + second_k)


def chain_solve(gathered, position):
    zero_line = jnp.zeros_like(gathered[0, 0])

    def forward(state_pair, column):
        carry_const, carry_slope = state_pair
        divisor = 1.0 - carry_slope * column[2]
        offset = (column[0] - column[2] * carry_const) / divisor
        slope = -column[4] / divisor
        next_const = column[1] - column[3] * (carry_const - carry_slope * column[0]) / divisor
        next_slope = column[5] + column[3] * carry_slope * column[4] / divisor
        return ((next_const, next_slope), (carry_const, carry_slope, offset, slope))

    _, (consts, slopes, offsets, gradients) = lax.scan(forward, (zero_line, zero_line), gathered)

    def backward(next_value, item):
        offset, slope, carry_const, carry_slope = item
        value = offset + slope * next_value
        return (value, (next_value, carry_const - carry_slope * value))

    _, (right_values, left_values) = lax.scan(
        backward, zero_line, (offsets, gradients, consts, slopes), reverse=True
    )
    left_value = lax.dynamic_index_in_dim(left_values, position, 0, keepdims=False)
    right_value = lax.dynamic_index_in_dim(right_values, position, 0, keepdims=False)
    return (left_value, right_value)


def interface_x(coeffs):
    gathered = lax.all_gather(coeffs[None], "gx", axis=0, tiled=True)
    return chain_solve(gathered, lax.axis_index("gx"))


def interface_y(coeffs):
    gathered = lax.all_gather(coeffs[None], "gy", axis=0, tiled=True)
    return chain_solve(gathered, lax.axis_index("gy"))


def interface_z(coeffs):
    gathered = lax.all_gather(coeffs[None], "gz", axis=0, tiled=True)
    return chain_solve(gathered, lax.axis_index("gz"))


def shifted(values, offset, axis, filler):
    length = values.shape[axis]
    pad_shape = list(values.shape)
    pad_shape[axis] = abs(offset)
    padding = jnp.full(tuple(pad_shape), filler, values.dtype)
    if offset > 0:
        return jnp.concatenate(
            [padding, lax.slice_in_dim(values, 0, length - offset, axis=axis)], axis=axis
        )
    return jnp.concatenate(
        [lax.slice_in_dim(values, -offset, length, axis=axis), padding], axis=axis
    )


def reduce_lines(right_side, face, axis, interface):
    length = right_side.shape[axis]
    low_face = lax.slice_in_dim(face, 0, length, axis=axis)
    high_face = lax.slice_in_dim(face, 1, length + 1, axis=axis)
    places = lax.broadcasted_iota(jnp.int32, right_side.shape, axis)
    lower_band = -IMPLICIT_WEIGHT * low_face
    upper_band = -IMPLICIT_WEIGHT * high_face
    main_band = 1.0 + IMPLICIT_WEIGHT * (low_face + high_face)
    left_side = jnp.where(places == 0, lower_band, 0.0)
    right_edge = jnp.where(places == length - 1, upper_band, 0.0)
    sub_band = jnp.where(places == 0, 0.0, lower_band)
    super_band = jnp.where(places == length - 1, 0.0, upper_band)
    sources = [right_side, left_side, right_edge]
    stride = 1
    while stride < length:
        sub_down = shifted(sub_band, stride, axis, 0.0)
        main_down = shifted(main_band, stride, axis, 1.0)
        super_down = shifted(super_band, stride, axis, 0.0)
        sub_up = shifted(sub_band, -stride, axis, 0.0)
        main_up = shifted(main_band, -stride, axis, 1.0)
        super_up = shifted(super_band, -stride, axis, 0.0)
        factor_down = -sub_band / main_down
        factor_up = -super_band / main_up
        sources = [
            source
            + factor_down * shifted(source, stride, axis, 0.0)
            + factor_up * shifted(source, -stride, axis, 0.0)
            for source in sources
        ]
        main_band = main_band + factor_down * super_down + factor_up * sub_up
        sub_band = factor_down * sub_down
        super_band = factor_up * super_up
        stride = stride * 2
    local_part, left_part, right_part = [source / main_band for source in sources]
    coeffs = jnp.stack(
        [
            lax.index_in_dim(local_part, 0, axis, keepdims=False),
            lax.index_in_dim(local_part, length - 1, axis, keepdims=False),
            lax.index_in_dim(left_part, 0, axis, keepdims=False),
            lax.index_in_dim(left_part, length - 1, axis, keepdims=False),
            lax.index_in_dim(right_part, 0, axis, keepdims=False),
            lax.index_in_dim(right_part, length - 1, axis, keepdims=False),
        ]
    )
    left_value, right_value = interface(coeffs)
    return (
        local_part
        - jnp.expand_dims(left_value, axis) * left_part
        - jnp.expand_dims(right_value, axis) * right_part
    )


def per_device(
    thermal_field,
    forcing_per_step,
    substance_label,
    thermal_conductivities,
    patch_group_label,
    drain_power_density,
):
    layer_voxel_number, height_voxel_number, width_voxel_number = thermal_field.shape
    voxel_thermal_link = jnp.zeros(thermal_field.shape, jnp.float32)
    for level in range(thermal_conductivities.shape[0]):
        voxel_thermal_link = voxel_thermal_link + jnp.where(
            substance_label == level, thermal_conductivities[level], 0.0
        )
    joined_outputs = jnp.stack([thermal_field, voxel_thermal_link])
    bordered_array = padded(joined_outputs, (("gx", 3), ("gy", 2), ("gz", 1)), 1)
    bordered_thermal_field = bordered_array[0]
    padk = bordered_array[1]
    sideways_link_xaxis = LATERAL_RATE * harmonic(padk[1:-1, 1:-1, :-1], padk[1:-1, 1:-1, 1:])
    sideways_link_yaxis = LATERAL_RATE * harmonic(padk[1:-1, :-1, 1:-1], padk[1:-1, 1:, 1:-1])
    upward_link_strength = VERTICAL_RATE * harmonic(padk[:-1, 1:-1, 1:-1], padk[1:, 1:-1, 1:-1])
    energy_current = sideways_link_xaxis[:, :, 1:] * (
        bordered_thermal_field[1:-1, 1:-1, 2:] - thermal_field
    ) - sideways_link_xaxis[:, :, :-1] * (thermal_field - bordered_thermal_field[1:-1, 1:-1, :-2])
    energy_current = (
        energy_current
        + sideways_link_yaxis[:, 1:, :] * (bordered_thermal_field[1:-1, 2:, 1:-1] - thermal_field)
        - sideways_link_yaxis[:, :-1, :] * (thermal_field - bordered_thermal_field[1:-1, :-2, 1:-1])
    )
    energy_current = (
        energy_current
        + upward_link_strength[1:] * (bordered_thermal_field[2:, 1:-1, 1:-1] - thermal_field)
        - upward_link_strength[:-1] * (thermal_field - bordered_thermal_field[:-2, 1:-1, 1:-1])
    )
    residual = SOURCE_STEP * forcing_per_step + energy_current
    step_x = reduce_lines(residual, sideways_link_xaxis, 2, interface_x)
    step_y = reduce_lines(step_x, sideways_link_yaxis, 1, interface_y)
    upward_correction = reduce_lines(step_y, upward_link_strength, 0, interface_z)
    next_thermal_field = thermal_field + upward_correction
    patch_extents = (
        layer_voxel_number,
        height_voxel_number // TY,
        TY,
        width_voxel_number // TX,
        TX,
    )
    patch_power_sum = next_thermal_field.reshape(patch_extents).sum(axis=(0, 2, 4)).reshape(-1)
    local_labels = patch_group_label.reshape(-1)
    cluster_count = drain_power_density.shape[0]
    onehot = (local_labels[:, None] == jnp.arange(cluster_count)[None, :]).astype(jnp.float32)
    partial_value = jnp.dot(patch_power_sum, onehot, precision=lax.Precision.HIGHEST)
    cluster_cells = 4 * layer_voxel_number * TY * TX
    cluster_total = lax.psum(partial_value, ("gx", "gy", "gz"))
    leak_power = drain_power_density * jnp.exp(LEAK_SLOPE * (cluster_total / cluster_cells))
    tile_power = jnp.dot(onehot, leak_power, precision=lax.Precision.HIGHEST)
    forcing_with_drain = forcing_per_step.reshape(patch_extents) + tile_power.reshape(
        1, height_voxel_number // TY, 1, width_voxel_number // TX, 1
    )
    return (next_thermal_field, forcing_with_drain.reshape(forcing_per_step.shape))


def solution(mesh):
    in_specs = (
        P("gz", "gy", "gx"),
        P("gz", "gy", "gx"),
        P("gz", "gy", "gx"),
        P(),
        P("gz", "gy", "gx"),
        P(),
    )
    out_specs = (P("gz", "gy", "gx"), P("gz", "gy", "gx"))
    return jax.shard_map(
        per_device, mesh=mesh, in_specs=in_specs, out_specs=out_specs, check_vma=False
    )
```

profile of v0, /device:TPU:0, one launch (start us, length us, event | category | flops | bytes accessed | tf_op | source)
XLA Modules:
  0.0 110.0 jit_solution(4359483157431193662)
XLA Ops:
  0.6 1.6 %fusion.115 = (f32[1]{0:T(128)}, f32[1]{0:T(128)}, f32[1]{0:T(128)}, f32[1]{0:T(128)}, f32[1]{0:T(128)}, /*index=5*/f32[1]{0:T(128)}, f32[1]{0:T(128)}, f32[1]{0:T(128)}) fusion(f32[8]{0:T(128)} %param.21), kind=kLoop, calls=%fused_computation.347 | loop fusion | bytes 64 | tf_op jit(solution)/shard_map/slice | solution.py:152
  2.3 5.9 %add_bitcast_fusion = f32[1,8,16,128]{3,2,1,0:T(8,128)S(1)} fusion(s32[8,16,128]{2,1,0:T(8,128)} %param.20, f32[]{:T(128)} %bitcast.8, f32[]{:T(128)} %bitcast.7, f32[]{:T(128)} %bitcast.6, f32[]{:T(128)} %bitcast.5, f32[]{:T(128)} %bitcast.4, f32[]{:T(128)} %bitcast.3, f32[]{:T(128)} %bitcast.2, f32[]{:T(128)} %bitcast.1), kind=kLoop, calls=%fused_computation.203 | loop fusion | flops 376832 | bytes 131104 | tf_op jit(solution)/shard_map/stack | solution.py:154
  8.3 4.8 %collective-permute-start = (f32[2,8,16,1]{3,2,1,0:T(8,128)S(1)}, f32[2,8,16,1]{3,2,1,0:T(8,128)S(1)}, u32[]{:S(2)}, u32[]{:S(2)}) collective-permute-start(f32[2,8,16,1]{3,2,1,0:T(8,128)S(1)} %get-tuple-element.1143), channel_id=1, source_target_pairs={{0,8},{8,16},{16,24},{1,9},{9,17},{17,25},{2,10},{10,18},{18,26},{... | collective-permute-start | bytes 3080 | tf_op jit(solution)/shard_map/ppermute | solution.py:22
  13.2 1.3 %collective-permute-start.1 = (f32[2,8,16,1]{3,2,1,0:T(8,128)S(1)}, f32[2,8,16,1]{3,2,1,0:T(8,128)S(1)}, u32[]{:S(2)}, u32[]{:S(2)}) collective-permute-start(f32[2,8,16,1]{3,2,1,0:T(8,128)S(1)} %get-tuple-element.1144), channel_id=1, source_target_pairs={{8,0},{16,8},{24,16},{9,1},{17,9},{25,17},{10,2},{18,10},{26,18},{... | collective-permute-start | bytes 3080 | tf_op jit(solution)/shard_map/ppermute | solution.py:23
  14.5 1.4 %collective-permute-done = f32[2,8,16,1]{3,2,1,0:T(8,128)S(1)} collective-permute-done((f32[2,8,16,1]{3,2,1,0:T(8,128)S(1)}, f32[2,8,16,1]{3,2,1,0:T(8,128)S(1)}, u32[]{:S(2)}, u32[]{:S(2)}) %collective-permute-start) | collective-permute-done | bytes 1056 | tf_op jit(solution)/shard_map/ppermute | solution.py:22
  15.9 4.8 %collective-permute-done.1 = f32[2,8,16,1]{3,2,1,0:T(8,128)S(1)} collective-permute-done((f32[2,8,16,1]{3,2,1,0:T(8,128)S(1)}, f32[2,8,16,1]{3,2,1,0:T(8,128)S(1)}, u32[]{:S(2)}, u32[]{:S(2)}) %collective-permute-start.1) | collective-permute-done | bytes 1056 | tf_op jit(solution)/shard_map/ppermute | solution.py:23
  20.7 0.2 pad_maximum_fusion.11
  20.8 1.3 %collective-permute-start.2 = (f32[2,8,1,130]{3,1,2,0:T(8,128)S(1)}, f32[2,8,1,130]{3,1,2,0:T(8,128)S(1)}, u32[]{:S(2)}, u32[]{:S(2)}) collective-permute-start(f32[2,8,1,130]{3,1,2,0:T(8,128)S(1)} %copy.710), channel_id=1, source_target_pairs={{0,4},{1,5},{2,6},{3,7},{8,12},{9,13},{10,14},{11,15},{16,20},{17,... | collective-permute-start | bytes 24968 | tf_op jit(solution)/shard_map/ppermute | solution.py:22
  22.2 1.3 %collective-permute-start.3 = (f32[2,8,1,130]{3,1,2,0:T(8,128)S(1)}, f32[2,8,1,130]{3,1,2,0:T(8,128)S(1)}, u32[]{:S(2)}, u32[]{:S(2)}) collective-permute-start(f32[2,8,1,130]{3,1,2,0:T(8,128)S(1)} %copy.711), channel_id=1, source_target_pairs={{4,0},{5,1},{6,2},{7,3},{12,8},{13,9},{14,10},{15,11},{20,16},{21,... | collective-permute-start | bytes 24968 | tf_op jit(solution)/shard_map/ppermute | solution.py:23
  23.5 1.7 %collective-permute-done.3 = f32[2,8,1,130]{3,1,2,0:T(8,128)S(1)} collective-permute-done((f32[2,8,1,130]{3,1,2,0:T(8,128)S(1)}, f32[2,8,1,130]{3,1,2,0:T(8,128)S(1)}, u32[]{:S(2)}, u32[]{:S(2)}) %collective-permute-start.3) | collective-permute-done | bytes 8352 | tf_op jit(solution)/shard_map/ppermute | solution.py:23
  25.4 3.5 %collective-permute-start.4 = (f32[2,1,18,130]{3,2,1,0:T(8,128)S(1)}, f32[2,1,18,130]{3,2,1,0:T(8,128)S(1)}, u32[]{:S(2)}, u32[]{:S(2)}) collective-permute-start(f32[2,1,18,130]{3,2,1,0:T(8,128)S(1)} %get-tuple-element.1066), channel_id=1, source_target_pairs={{0,1},{1,2},{2,3},{4,5},{5,6},{6,7},{8,9},{9,10},{10,11},{12,13},{... | collective-permute-start | bytes 56168 | tf_op jit(solution)/shard_map/ppermute | solution.py:22
  28.9 1.3 %collective-permute-start.5 = (f32[2,1,18,130]{3,2,1,0:T(8,128)S(1)}, f32[2,1,18,130]{3,2,1,0:T(8,128)S(1)}, u32[]{:S(2)}, u32[]{:S(2)}) collective-permute-start(f32[2,1,18,130]{3,2,1,0:T(8,128)S(1)} %get-tuple-element.1067), channel_id=1, source_target_pairs={{1,0},{2,1},{3,2},{5,4},{6,5},{7,6},{9,8},{10,9},{11,10},{13,12},{... | collective-permute-start | bytes 56168 | tf_op jit(solution)/shard_map/ppermute | solution.py:23
  30.3 0.7 copy-done.2
  31.0 3.8 %collective-permute-done.5 = f32[2,1,18,130]{3,2,1,0:T(8,128)S(1)} collective-permute-done((f32[2,1,18,130]{3,2,1,0:T(8,128)S(1)}, f32[2,1,18,130]{3,2,1,0:T(8,128)S(1)}, u32[]{:S(2)}, u32[]{:S(2)}) %collective-permute-start.5) | collective-permute-done | bytes 18752 | tf_op jit(solution)/shard_map/ppermute | solution.py:23
  34.8 0.2 pad_maximum_fusion
  35.1 0.1 divide_multiply_fusion.1
  35.2 0.1 divide_multiply_fusion
  35.4 0.1 divide_multiply_fusion.2
  35.8 0.8 copy-done.1
  36.6 0.2 fusion.14
  37.0 0.1 multiply_add_fusion.35
  37.6 0.2 multiply_add_fusion.48
  38.4 0.2 multiply_add_fusion.46
  39.2 0.2 multiply_add_fusion.44
  40.0 0.2 multiply_add_fusion.42
  40.8 0.2 multiply_add_fusion.40
  41.3 0.1 multiply_add_fusion.38
  41.7 0.1 add_divide_fusion.8
  41.8 0.2 slice_reduce_fusion.4
  42.2 0.2 add_divide_fusion.7
  42.3 0.2 slice_reduce_fusion.2
  42.5 0.2 slice_reduce_fusion
  42.7 8.6 %all-gather = f32[24,8,16]{2,1,0:T(8,128)S(1)} all-gather(f32[6,8,16]{2,1,0:T(8,128)S(1)} %constant_dynamic-update-slice_fusion), channel_id=2, replica_groups=mesh['gx'=4,'gy'=2,'gz'=4] {'gx'}, dimensions={0}, use_global_device_ids=true | all-gather | bytes 15360 | tf_op jit(solution)/shard_map/all_gather | solution.py:60
  51.4 0.3 while.120
  51.7 0.1 while.121
  52.1 0.1 multiply_add_fusion.22
  52.3 0.1 multiply_add_fusion.20
  52.9 1.8 %all-gather.1 = f32[12,8,128]{2,1,0:T(8,128)S(1)} all-gather(f32[6,8,128]{2,1,0:T(8,128)S(1)} %constant_dynamic-update-slice_fusion.6), channel_id=3, replica_groups=mesh['gx'=4,'gy'=2,'gz'=4] {'gy'}, dimensions={0}, use_global_device_ids=true | all-gather | bytes 73728 | tf_op jit(solution)/shard_map/all_gather | solution.py:65
  54.8 0.1 while.122
  55.2 0.1 multiply_add_fusion.3
  55.9 13.8 %all-gather.2 = f32[24,16,128]{2,1,0:T(8,128)S(1)} all-gather(f32[6,16,128]{2,1,0:T(8,128)S(1)} %constant_dynamic-update-slice_fusion.12), channel_id=4, replica_groups=mesh['gx'=4,'gy'=2,'gz'=4] {'gz'}, dimensions={0}, use_global_device_ids=true | all-gather | bytes 245760 | tf_op jit(solution)/shard_map/all_gather | solution.py:70
  69.7 0.3 while.124
  70.1 0.1 while.125
  70.3 0.7 fusion.33
  71.2 0.2 convolution_bitcast_fusion.1
  71.4 37.5 %psum.7 = f32[64]{0:T(128)S(1)} all-reduce(f32[64]{0:T(128)S(1)} %convolution_bitcast_fusion.1), channel_id=1, replica_groups=mesh['gx'=4,'gy'=2,'gz'=4] {'gx','gy','gz'}, use_global_device_ids=true, to_apply=%region_14.15 | all-reduce | flops 64 | bytes 512 | tf_op jit(solution)/shard_map/psum | solution.py:192
  108.9 0.2 convolution_bitcast_fusion
  109.3 0.6 broadcast_add_fusion
  (213 shorter events, 6.9 us)
Async XLA Ops:
  2.3 5.9 %copy-start = (f32[8,16,128]{2,1,0:T(8,128)S(1)}, f32[8,16,128]{2,1,0:T(8,128)}, u32[]{:S(2)}) copy-start(f32[8,16,128]{2,1,0:T(8,128)} %param.18) | copy-start | bytes 196612
  8.3 7.6 %collective-permute-start = (f32[2,8,16,1]{3,2,1,0:T(8,128)S(1)}, f32[2,8,16,1]{3,2,1,0:T(8,128)S(1)}, u32[]{:S(2)}, u32[]{:S(2)}) collective-permute-start(f32[2,8,16,1]{3,2,1,0:T(8,128)S(1)} %get-tuple-element.1143), channel_id=1, source_target_pairs={{0,8},{8,16},{16,24},{1,9},{9,17},{17,25},{2,10},{10,18},{18,26},{... | collective-permute-start | bytes 3080 | tf_op jit(solution)/shard_map/ppermute | solution.py:22
  13.2 7.5 %collective-permute-start.1 = (f32[2,8,16,1]{3,2,1,0:T(8,128)S(1)}, f32[2,8,16,1]{3,2,1,0:T(8,128)S(1)}, u32[]{:S(2)}, u32[]{:S(2)}) collective-permute-start(f32[2,8,16,1]{3,2,1,0:T(8,128)S(1)} %get-tuple-element.1144), channel_id=1, source_target_pairs={{8,0},{16,8},{24,16},{9,1},{17,9},{25,17},{10,2},{18,10},{26,18},{... | collective-permute-start | bytes 3080 | tf_op jit(solution)/shard_map/ppermute | solution.py:23
  20.8 2.6 %collective-permute-start.2 = (f32[2,8,1,130]{3,1,2,0:T(8,128)S(1)}, f32[2,8,1,130]{3,1,2,0:T(8,128)S(1)}, u32[]{:S(2)}, u32[]{:S(2)}) collective-permute-start(f32[2,8,1,130]{3,1,2,0:T(8,128)S(1)} %copy.710), channel_id=1, source_target_pairs={{0,4},{1,5},{2,6},{3,7},{8,12},{9,13},{10,14},{11,15},{16,20},{17,... | collective-permute-start | bytes 24968 | tf_op jit(solution)/shard_map/ppermute | solution.py:22
  22.2 3.1 %collective-permute-start.3 = (f32[2,8,1,130]{3,1,2,0:T(8,128)S(1)}, f32[2,8,1,130]{3,1,2,0:T(8,128)S(1)}, u32[]{:S(2)}, u32[]{:S(2)}) collective-permute-start(f32[2,8,1,130]{3,1,2,0:T(8,128)S(1)} %copy.711), channel_id=1, source_target_pairs={{4,0},{5,1},{6,2},{7,3},{12,8},{13,9},{14,10},{15,11},{20,16},{21,... | collective-permute-start | bytes 24968 | tf_op jit(solution)/shard_map/ppermute | solution.py:23
  25.4 5.7 %collective-permute-start.4 = (f32[2,1,18,130]{3,2,1,0:T(8,128)S(1)}, f32[2,1,18,130]{3,2,1,0:T(8,128)S(1)}, u32[]{:S(2)}, u32[]{:S(2)}) collective-permute-start(f32[2,1,18,130]{3,2,1,0:T(8,128)S(1)} %get-tuple-element.1066), channel_id=1, source_target_pairs={{0,1},{1,2},{2,3},{4,5},{5,6},{6,7},{8,9},{9,10},{10,11},{12,13},{... | collective-permute-start | bytes 56168 | tf_op jit(solution)/shard_map/ppermute | solution.py:22
  28.9 6.0 %collective-permute-start.5 = (f32[2,1,18,130]{3,2,1,0:T(8,128)S(1)}, f32[2,1,18,130]{3,2,1,0:T(8,128)S(1)}, u32[]{:S(2)}, u32[]{:S(2)}) collective-permute-start(f32[2,1,18,130]{3,2,1,0:T(8,128)S(1)} %get-tuple-element.1067), channel_id=1, source_target_pairs={{1,0},{2,1},{3,2},{5,4},{6,5},{7,6},{9,8},{10,9},{11,10},{13,12},{... | collective-permute-start | bytes 56168 | tf_op jit(solution)/shard_map/ppermute | solution.py:23
  30.3 0.7 copy-start.2
  35.8 0.8 copy-start.1
  71.4 37.5 %copy-start.3 = (f32[64]{0:T(128)S(1)}, f32[64]{0:T(128)}, u32[]{:S(2)}) copy-start(f32[64]{0:T(128)} %param.23) | copy-start | bytes 772
where the time goes:
time: 111 us; the launch traced here: 110 us
  blocking collectives  61.8 us (56%)
  starting transfers between devices  13.5 us (12%)
  other arithmetic  12.2 us (11%)
  waiting for transfers between devices  11.7 us (11%)
  local copies, waits for them, and re-layouts  8.1 us (7%)
  between operations  1.81 us (2%)
    psum x1, blocking collectives, per_device(): cluster_total = lax.psum(partial_value, ('gx', 'gy', 'gz'))  37.5 us
    all_gather x1, blocking collectives, interface_z(): gathered = lax.all_gather(coeffs[None], 'gz', axis=0, tiled=True)  13.8 us
    ppermute x3, waiting for transfers between devices, padded(): after = lax.ppermute(first, axis, down)  10.3 us
    ppermute x3, starting transfers between devices, padded(): before = lax.ppermute(last, axis, up)  9.62 us
    all_gather x1, blocking collectives, interface_x(): gathered = lax.all_gather(coeffs[None], 'gx', axis=0, tiled=True)  8.61 us
    another operation x2, other arithmetic, per_device(): joined_outputs = jnp.stack([thermal_field, voxel_thermal_link])  6.03 us
    ppermute x3, starting transfers between devices, padded(): after = lax.ppermute(first, axis, down)  3.88 us
    slice x50, local copies, waits for them, and re-layouts, shifted(): lax.slice_in_dim(values, 0, length - offset, axis=axis)  2.41 us
  transfers between devices with their start and end apart: 6, of which 4 were waited for; matrix products, arithmetic and copies ran while one was open for 0% of the time, Pallas kernels for 0%

commit v1 on v0

--- a/solution.py
+++ b/solution.py
@@ -1,3 +1,4 @@
+import functools
 import jax
 import jax.numpy as jnp
 from jax import lax
@@ -10,6 +11,15 @@
 VERTICAL_RATE = 400.0
 SOURCE_STEP = 0.5
 LEAK_SLOPE = 0.5
+
+
+def lead_members_all(vector, device_axis, net_axis):
+    for no in (device_axis, net_axis):
+        vector = lax.psum(vector, axis_name=no)
+    return vector
+
+
+recast_heaps = functools.partial(lead_members_all, device_axis=("gy", "gz"), net_axis="gx")
 
 
 def padded(shard, sides, width):
@@ -189,7 +199,7 @@
     onehot = (local_labels[:, None] == jnp.arange(cluster_count)[None, :]).astype(jnp.float32)
     partial_value = jnp.dot(patch_power_sum, onehot, precision=lax.Precision.HIGHEST)
     cluster_cells = 4 * layer_voxel_number * TY * TX
-    cluster_total = lax.psum(partial_value, ("gx", "gy", "gz"))
+    cluster_total = recast_heaps(partial_value)
     leak_power = drain_power_density * jnp.exp(LEAK_SLOPE * (cluster_total / cluster_cells))
     tile_power = jnp.dot(onehot, leak_power, precision=lax.Precision.HIGHEST)
     forcing_with_drain = forcing_per_step.reshape(patch_extents) + tile_power.reshape(

time: 111 us -> 95.7 us (0.86)
  blocking collectives: 61.8 us -> 46.9 us
    psum x1 -> x2, blocking collectives: 37.5 us -> 22.6 us  [lead_members_all(): vector = lax.psum(vector, axis_name=no)]
where the time goes in v1:
time: 95.7 us; the launch traced here: 95.1 us
  blocking collectives  46.9 us (49%)
  starting transfers between devices  13.5 us (14%)
  other arithmetic  12.3 us (13%)
  waiting for transfers between devices  11.7 us (12%)
  local copies, waits for them, and re-layouts  8.08 us (8%)
  between operations  1.82 us (2%)
    psum x2, blocking collectives, lead_members_all(): vector = lax.psum(vector, axis_name=no)  22.6 us
    all_gather x1, blocking collectives, interface_z(): gathered = lax.all_gather(coeffs[None], 'gz', axis=0, tiled=True)  13.8 us
    ppermute x3, waiting for transfers between devices, padded(): after = lax.ppermute(first, axis, down)  10.3 us
    ppermute x3, starting transfers between devices, padded(): before = lax.ppermute(last, axis, up)  9.62 us
    all_gather x1, blocking collectives, interface_x(): gathered = lax.all_gather(coeffs[None], 'gx', axis=0, tiled=True)  8.61 us
    another operation x2, other arithmetic, per_device(): joined_outputs = jnp.stack([thermal_field, voxel_thermal_link])  6.1 us
    ppermute x3, starting transfers between devices, padded(): after = lax.ppermute(first, axis, down)  3.88 us
    slice x50, local copies, waits for them, and re-layouts, shifted(): lax.slice_in_dim(values, 0, length - offset, axis=axis)  2.41 us
  transfers between devices with their start and end apart: 6, of which 4 were waited for; matrix products, arithmetic and copies ran while one was open for 0% of the time, Pallas kernels for 0%

profile of v1, /device:TPU:0, one launch (start us, length us, event | category | flops | bytes accessed | tf_op | source)
XLA Modules:
  0.0 95.1 jit_solution(9688698769205649540)
XLA Ops:
  0.6 1.6 %fusion.115 = (f32[1]{0:T(128)}, f32[1]{0:T(128)}, f32[1]{0:T(128)}, f32[1]{0:T(128)}, f32[1]{0:T(128)}, /*index=5*/f32[1]{0:T(128)}, f32[1]{0:T(128)}, f32[1]{0:T(128)}) fusion(f32[8]{0:T(128)} %param.21), kind=kLoop, calls=%fused_computation.347 | loop fusion | bytes 64 | tf_op jit(solution)/shard_map/slice | solution.py:162
  2.3 6.0 %add_bitcast_fusion = f32[1,8,16,128]{3,2,1,0:T(8,128)S(1)} fusion(s32[8,16,128]{2,1,0:T(8,128)} %param.20, f32[]{:T(128)} %bitcast.8, f32[]{:T(128)} %bitcast.7, f32[]{:T(128)} %bitcast.6, f32[]{:T(128)} %bitcast.5, f32[]{:T(128)} %bitcast.4, f32[]{:T(128)} %bitcast.3, f32[]{:T(128)} %bitcast.2, f32[]{:T(128)} %bitcast.1), kind=kLoop, calls=%fused_computation.203 | loop fusion | flops 376832 | bytes 131104 | tf_op jit(solution)/shard_map/stack | solution.py:164
  8.4 4.8 %collective-permute-start = (f32[2,8,16,1]{3,2,1,0:T(8,128)S(1)}, f32[2,8,16,1]{3,2,1,0:T(8,128)S(1)}, u32[]{:S(2)}, u32[]{:S(2)}) collective-permute-start(f32[2,8,16,1]{3,2,1,0:T(8,128)S(1)} %get-tuple-element.1143), channel_id=1, source_target_pairs={{0,8},{8,16},{16,24},{1,9},{9,17},{17,25},{2,10},{10,18},{18,26},{... | collective-permute-start | bytes 3080 | tf_op jit(solution)/shard_map/ppermute | solution.py:32
  13.2 1.3 %collective-permute-start.1 = (f32[2,8,16,1]{3,2,1,0:T(8,128)S(1)}, f32[2,8,16,1]{3,2,1,0:T(8,128)S(1)}, u32[]{:S(2)}, u32[]{:S(2)}) collective-permute-start(f32[2,8,16,1]{3,2,1,0:T(8,128)S(1)} %get-tuple-element.1144), channel_id=1, source_target_pairs={{8,0},{16,8},{24,16},{9,1},{17,9},{25,17},{10,2},{18,10},{26,18},{... | collective-permute-start | bytes 3080 | tf_op jit(solution)/shard_map/ppermute | solution.py:33
  14.6 1.4 %collective-permute-done = f32[2,8,16,1]{3,2,1,0:T(8,128)S(1)} collective-permute-done((f32[2,8,16,1]{3,2,1,0:T(8,128)S(1)}, f32[2,8,16,1]{3,2,1,0:T(8,128)S(1)}, u32[]{:S(2)}, u32[]{:S(2)}) %collective-permute-start) | collective-permute-done | bytes 1056 | tf_op jit(solution)/shard_map/ppermute | solution.py:32
  16.0 4.8 %collective-permute-done.1 = f32[2,8,16,1]{3,2,1,0:T(8,128)S(1)} collective-permute-done((f32[2,8,16,1]{3,2,1,0:T(8,128)S(1)}, f32[2,8,16,1]{3,2,1,0:T(8,128)S(1)}, u32[]{:S(2)}, u32[]{:S(2)}) %collective-permute-start.1) | collective-permute-done | bytes 1056 | tf_op jit(solution)/shard_map/ppermute | solution.py:33
  20.7 0.2 pad_maximum_fusion.11
  20.9 1.3 %collective-permute-start.2 = (f32[2,8,1,130]{3,1,2,0:T(8,128)S(1)}, f32[2,8,1,130]{3,1,2,0:T(8,128)S(1)}, u32[]{:S(2)}, u32[]{:S(2)}) collective-permute-start(f32[2,8,1,130]{3,1,2,0:T(8,128)S(1)} %copy.710), channel_id=1, source_target_pairs={{0,4},{1,5},{2,6},{3,7},{8,12},{9,13},{10,14},{11,15},{16,20},{17,... | collective-permute-start | bytes 24968 | tf_op jit(solution)/shard_map/ppermute | solution.py:32
  22.2 1.3 %collective-permute-start.3 = (f32[2,8,1,130]{3,1,2,0:T(8,128)S(1)}, f32[2,8,1,130]{3,1,2,0:T(8,128)S(1)}, u32[]{:S(2)}, u32[]{:S(2)}) collective-permute-start(f32[2,8,1,130]{3,1,2,0:T(8,128)S(1)} %copy.711), channel_id=1, source_target_pairs={{4,0},{5,1},{6,2},{7,3},{12,8},{13,9},{14,10},{15,11},{20,16},{21,... | collective-permute-start | bytes 24968 | tf_op jit(solution)/shard_map/ppermute | solution.py:33
  23.6 1.7 %collective-permute-done.3 = f32[2,8,1,130]{3,1,2,0:T(8,128)S(1)} collective-permute-done((f32[2,8,1,130]{3,1,2,0:T(8,128)S(1)}, f32[2,8,1,130]{3,1,2,0:T(8,128)S(1)}, u32[]{:S(2)}, u32[]{:S(2)}) %collective-permute-start.3) | collective-permute-done | bytes 8352 | tf_op jit(solution)/shard_map/ppermute | solution.py:33
  25.4 3.5 %collective-permute-start.4 = (f32[2,1,18,130]{3,2,1,0:T(8,128)S(1)}, f32[2,1,18,130]{3,2,1,0:T(8,128)S(1)}, u32[]{:S(2)}, u32[]{:S(2)}) collective-permute-start(f32[2,1,18,130]{3,2,1,0:T(8,128)S(1)} %get-tuple-element.1066), channel_id=1, source_target_pairs={{0,1},{1,2},{2,3},{4,5},{5,6},{6,7},{8,9},{9,10},{10,11},{12,13},{... | collective-permute-start | bytes 56168 | tf_op jit(solution)/shard_map/ppermute | solution.py:32
  28.9 1.3 %collective-permute-start.5 = (f32[2,1,18,130]{3,2,1,0:T(8,128)S(1)}, f32[2,1,18,130]{3,2,1,0:T(8,128)S(1)}, u32[]{:S(2)}, u32[]{:S(2)}) collective-permute-start(f32[2,1,18,130]{3,2,1,0:T(8,128)S(1)} %get-tuple-element.1067), channel_id=1, source_target_pairs={{1,0},{2,1},{3,2},{5,4},{6,5},{7,6},{9,8},{10,9},{11,10},{13,12},{... | collective-permute-start | bytes 56168 | tf_op jit(solution)/shard_map/ppermute | solution.py:33
  30.3 0.7 copy-done.2
  31.1 3.8 %collective-permute-done.5 = f32[2,1,18,130]{3,2,1,0:T(8,128)S(1)} collective-permute-done((f32[2,1,18,130]{3,2,1,0:T(8,128)S(1)}, f32[2,1,18,130]{3,2,1,0:T(8,128)S(1)}, u32[]{:S(2)}, u32[]{:S(2)}) %collective-permute-start.5) | collective-permute-done | bytes 18752 | tf_op jit(solution)/shard_map/ppermute | solution.py:33
  34.9 0.2 pad_maximum_fusion
  35.2 0.1 divide_multiply_fusion.1
  35.3 0.1 divide_multiply_fusion
  35.4 0.1 divide_multiply_fusion.2
  35.8 0.8 copy-done.1
  36.7 0.2 fusion.14
  37.0 0.1 multiply_add_fusion.35
  37.7 0.2 multiply_add_fusion.48
  38.5 0.2 multiply_add_fusion.46
  39.2 0.2 multiply_add_fusion.44
  40.0 0.2 multiply_add_fusion.42
  40.8 0.2 multiply_add_fusion.40
  41.3 0.1 multiply_add_fusion.38
  41.7 0.1 add_divide_fusion.8
  41.9 0.2 slice_reduce_fusion.4
  42.2 0.2 add_divide_fusion.7
  42.4 0.2 slice_reduce_fusion.2
  42.6 0.2 slice_reduce_fusion
  42.8 8.6 %all-gather = f32[24,8,16]{2,1,0:T(8,128)S(1)} all-gather(f32[6,8,16]{2,1,0:T(8,128)S(1)} %constant_dynamic-update-slice_fusion), channel_id=2, replica_groups=mesh['gx'=4,'gy'=2,'gz'=4] {'gx'}, dimensions={0}, use_global_device_ids=true | all-gather | bytes 15360 | tf_op jit(solution)/shard_map/all_gather | solution.py:70
  51.4 0.3 while.120
  51.8 0.1 while.121
  52.1 0.1 multiply_add_fusion.22
  52.4 0.1 multiply_add_fusion.20
  53.0 1.8 %all-gather.1 = f32[12,8,128]{2,1,0:T(8,128)S(1)} all-gather(f32[6,8,128]{2,1,0:T(8,128)S(1)} %constant_dynamic-update-slice_fusion.6), channel_id=3, replica_groups=mesh['gx'=4,'gy'=2,'gz'=4] {'gy'}, dimensions={0}, use_global_device_ids=true | all-gather | bytes 73728 | tf_op jit(solution)/shard_map/all_gather | solution.py:75
  54.8 0.1 while.122
  55.9 13.8 %all-gather.2 = f32[24,16,128]{2,1,0:T(8,128)S(1)} all-gather(f32[6,16,128]{2,1,0:T(8,128)S(1)} %constant_dynamic-update-slice_fusion.12), channel_id=4, replica_groups=mesh['gx'=4,'gy'=2,'gz'=4] {'gz'}, dimensions={0}, use_global_device_ids=true | all-gather | bytes 245760 | tf_op jit(solution)/shard_map/all_gather | solution.py:80
  69.8 0.3 while.124
  70.1 0.1 while.125
  70.3 0.7 fusion.33
  71.2 0.2 convolution_bitcast_fusion.1
  71.4 13.7 %psum.14 = f32[64]{0:T(128)S(1)} all-reduce(f32[64]{0:T(128)S(1)} %convolution_bitcast_fusion.1), channel_id=1, replica_groups=mesh['gx'=4,'gy'=2,'gz'=4] {'gy','gz'}, use_global_device_ids=true, to_apply=%region_14.15 | all-reduce | flops 64 | bytes 512 | tf_op jit(solution)/shard_map/psum | solution.py:18
  85.1 8.9 %psum.15 = f32[64]{0:T(128)S(1)} all-reduce(f32[64]{0:T(128)S(1)} %psum.14), channel_id=1, replica_groups=mesh['gx'=4,'gy'=2,'gz'=4] {'gx'}, use_global_device_ids=true, to_apply=%region_15.16 | all-reduce | flops 64 | bytes 512 | tf_op jit(solution)/shard_map/psum | solution.py:18
  94.0 0.2 convolution_bitcast_fusion
  94.5 0.6 broadcast_add_fusion
  (214 shorter events, 7.0 us)
Async XLA Ops:
  2.2 6.0 %copy-start = (f32[8,16,128]{2,1,0:T(8,128)S(1)}, f32[8,16,128]{2,1,0:T(8,128)}, u32[]{:S(2)}) copy-start(f32[8,16,128]{2,1,0:T(8,128)} %param.18) | copy-start | bytes 196612
  8.4 7.6 %collective-permute-start = (f32[2,8,16,1]{3,2,1,0:T(8,128)S(1)}, f32[2,8,16,1]{3,2,1,0:T(8,128)S(1)}, u32[]{:S(2)}, u32[]{:S(2)}) collective-permute-start(f32[2,8,16,1]{3,2,1,0:T(8,128)S(1)} %get-tuple-element.1143), channel_id=1, source_target_pairs={{0,8},{8,16},{16,24},{1,9},{9,17},{17,25},{2,10},{10,18},{18,26},{... | collective-permute-start | bytes 3080 | tf_op jit(solution)/shard_map/ppermute | solution.py:32
  13.2 7.5 %collective-permute-start.1 = (f32[2,8,16,1]{3,2,1,0:T(8,128)S(1)}, f32[2,8,16,1]{3,2,1,0:T(8,128)S(1)}, u32[]{:S(2)}, u32[]{:S(2)}) collective-permute-start(f32[2,8,16,1]{3,2,1,0:T(8,128)S(1)} %get-tuple-element.1144), channel_id=1, source_target_pairs={{8,0},{16,8},{24,16},{9,1},{17,9},{25,17},{10,2},{18,10},{26,18},{... | collective-permute-start | bytes 3080 | tf_op jit(solution)/shard_map/ppermute | solution.py:33
  20.9 2.6 %collective-permute-start.2 = (f32[2,8,1,130]{3,1,2,0:T(8,128)S(1)}, f32[2,8,1,130]{3,1,2,0:T(8,128)S(1)}, u32[]{:S(2)}, u32[]{:S(2)}) collective-permute-start(f32[2,8,1,130]{3,1,2,0:T(8,128)S(1)} %copy.710), channel_id=1, source_target_pairs={{0,4},{1,5},{2,6},{3,7},{8,12},{9,13},{10,14},{11,15},{16,20},{17,... | collective-permute-start | bytes 24968 | tf_op jit(solution)/shard_map/ppermute | solution.py:32
  22.2 3.1 %collective-permute-start.3 = (f32[2,8,1,130]{3,1,2,0:T(8,128)S(1)}, f32[2,8,1,130]{3,1,2,0:T(8,128)S(1)}, u32[]{:S(2)}, u32[]{:S(2)}) collective-permute-start(f32[2,8,1,130]{3,1,2,0:T(8,128)S(1)} %copy.711), channel_id=1, source_target_pairs={{4,0},{5,1},{6,2},{7,3},{12,8},{13,9},{14,10},{15,11},{20,16},{21,... | collective-permute-start | bytes 24968 | tf_op jit(solution)/shard_map/ppermute | solution.py:33
  25.4 5.7 %collective-permute-start.4 = (f32[2,1,18,130]{3,2,1,0:T(8,128)S(1)}, f32[2,1,18,130]{3,2,1,0:T(8,128)S(1)}, u32[]{:S(2)}, u32[]{:S(2)}) collective-permute-start(f32[2,1,18,130]{3,2,1,0:T(8,128)S(1)} %get-tuple-element.1066), channel_id=1, source_target_pairs={{0,1},{1,2},{2,3},{4,5},{5,6},{6,7},{8,9},{9,10},{10,11},{12,13},{... | collective-permute-start | bytes 56168 | tf_op jit(solution)/shard_map/ppermute | solution.py:32
  28.9 6.0 %collective-permute-start.5 = (f32[2,1,18,130]{3,2,1,0:T(8,128)S(1)}, f32[2,1,18,130]{3,2,1,0:T(8,128)S(1)}, u32[]{:S(2)}, u32[]{:S(2)}) collective-permute-start(f32[2,1,18,130]{3,2,1,0:T(8,128)S(1)} %get-tuple-element.1067), channel_id=1, source_target_pairs={{1,0},{2,1},{3,2},{5,4},{6,5},{7,6},{9,8},{10,9},{11,10},{13,12},{... | collective-permute-start | bytes 56168 | tf_op jit(solution)/shard_map/ppermute | solution.py:33
  30.3 0.7 copy-start.2
  35.8 0.8 copy-start.1
  85.1 8.9 %copy-start.3 = (f32[64]{0:T(128)S(1)}, f32[64]{0:T(128)}, u32[]{:S(2)}) copy-start(f32[64]{0:T(128)} %param.23) | copy-start | bytes 772
